TPU v7x, 32 devices: a whole 2x2x4 slice. The times are simulated.
32 devices in a mesh: fsdp: 4 (over x, core), context: 4 (over z), tensor: 2 (over y).
Axes of the slice: x: 2, y: 2, z: 4, core: 2. Of those that a mesh axis runs over, the one named last changes fastest.
Arguments:
- tokens: bfloat16 [32, 1024, 1024], P('fsdp', 'context'), may hold values from -6 to 6
- segments: int32 [32, 1024], P('fsdp'), may hold values from 0 to 4, as said below
- input_gain: bfloat16 [1024], P('fsdp'), may hold values from 0.25 to 1.75
- middle_gain: bfloat16 [1024], P('fsdp'), may hold values from 0.25 to 1.75
- query_gain: bfloat16 [128], P('fsdp'), may hold values from 0.25 to 1.75
- key_gain: bfloat16 [128], P('fsdp'), may hold values from 0.25 to 1.75
- w_query: bfloat16 [1024, 2048], P('fsdp', 'tensor'), may hold values from -0.1875 to 0.1875
- key_projection_weight: bfloat16 [1024, 1024], P('fsdp', 'tensor'), may hold values from -0.1875 to 0.1875
- value_projection_weight: bfloat16 [1024, 1024], P('fsdp', 'tensor'), may hold values from -0.1875 to 0.1875
- w_out: bfloat16 [2048, 1024], P('tensor', 'fsdp'), may hold values from -1.5 to 1.5
- w_gate: bfloat16 [1024, 3072], P('fsdp', 'tensor'), may hold values from -0.1875 to 0.1875
- w_up: bfloat16 [1024, 3072], P('fsdp', 'tensor'), may hold values from -0.1875 to 0.1875
- w_down: bfloat16 [3072, 1024], P('tensor', 'fsdp'), may hold values from -0.109375 to 0.109375
- cotangent: bfloat16 [32, 1024, 1024], P('fsdp', 'context'), may hold values from -6 to 6
Outputs:
- block_out: bfloat16 [32, 1024, 1024], P('fsdp', 'context')
- grad_tokens: bfloat16 [32, 1024, 1024], P('fsdp', 'context')
- grad_input_gain: float32 [1024], P('fsdp')
- grad_middle_gain: float32 [1024], P('fsdp')
- grad_query_gain: float32 [128], P('fsdp')
- grad_key_gain: float32 [128], P('fsdp')
- grad_w_query: float32 [1024, 2048], P('fsdp', 'tensor')
- grad_w_key: float32 [1024, 1024], P('fsdp', 'tensor')
- grad_w_value: float32 [1024, 1024], P('fsdp', 'tensor')
- grad_w_out: float32 [2048, 1024], P('tensor', 'fsdp')
- grad_w_gate: float32 [1024, 3072], P('fsdp', 'tensor')
- grad_w_up: float32 [1024, 3072], P('fsdp', 'tensor')
- grad_w_down: float32 [3072, 1024], P('tensor', 'fsdp')
Inputs may be any that keep to these rules, and one draw needn't show every extreme that they name: `segments`: within each sequence the segment numbers start at 0 and never fall. In each aligned block of 8 sequences (those of one index of fsdp) exactly one sequence is a single document, and every other sequence holds exactly five documents.
All inputs are finite; a program needn't handle non-finite values.
Results may differ from a plain program's by a relative error of at most 0.023.
Values may be sent and summed in bfloat16 or wider, within the bound.
No kernel may reach another device: no remote copies, remote signals or barrier semaphores. Data moves between devices by JAX's collectives and lax.ppermute only.
A program may use at most 320 MiB of HBM per device.

v0:
```python
import math

import jax
import jax.numpy as jnp
from jax import lax
from jax.sharding import PartitionSpec as P

EPS = 1e-06
THETA = 1000000.0
MASKED = -1000000000.0


def rms_factor(values):
    return lax.rsqrt(jnp.mean(values * values, axis=-1, keepdims=True) + EPS)


def rms_backward(grad_out, normed, factor, gain_vec):
    scaled = grad_out * gain_vec
    return factor * (scaled - normed * jnp.mean(scaled * normed, axis=-1, keepdims=True))


def doc_positions(segments):
    sequence_length = segments.shape[-1]
    places = jnp.arange(sequence_length, dtype=jnp.int32)
    earlier = jnp.concatenate([segments[:, :1], segments[:, :-1]], axis=1)
    starts = jnp.where(segments != earlier, places[None, :], 0)
    return places[None, :] - lax.cummax(starts, axis=1)


def rotary_tables(positions, head_dim):
    half_dim = head_dim // 2
    frequencies = THETA ** (-(2.0 * jnp.arange(half_dim, dtype=jnp.float32)) / head_dim)
    angles = positions.astype(jnp.float32)[..., None] * frequencies
    return (jnp.cos(angles), jnp.sin(angles))


def rotate(values, rot_cos, rot_sin, direction):
    half_dim = values.shape[-1] // 2
    front_half = values[..., :half_dim]
    back_half = values[..., half_dim:]
    return jnp.concatenate(
        [
            front_half * rot_cos - direction * back_half * rot_sin,
            back_half * rot_cos + direction * front_half * rot_sin,
        ],
        axis=-1,
    )


def block_group(seq_count, local_len):
    block_share = 1
    for candidate in range(1, seq_count + 1):
        if seq_count % candidate == 0 and candidate * local_len <= 512:
            block_share = candidate
    return block_share


def local(
    tokens,
    segments,
    input_gain,
    middle_gain,
    query_gain,
    key_gain,
    w_query,
    key_projection_weight,
    value_projection_weight,
    w_out,
    w_gate,
    w_up,
    w_down,
    cotangent,
):
    (
        input_gain,
        middle_gain,
        query_gain,
        key_gain,
        w_query,
        key_projection_weight,
        value_projection_weight,
        w_out,
        w_gate,
        w_up,
        w_down,
    ) = (
        lax.all_gather(input_gain, "fsdp", axis=0, tiled=True),
        lax.all_gather(middle_gain, "fsdp", axis=0, tiled=True),
        lax.all_gather(query_gain, "fsdp", axis=0, tiled=True),
        lax.all_gather(key_gain, "fsdp", axis=0, tiled=True),
        lax.all_gather(w_query, "fsdp", axis=0, tiled=True),
        lax.all_gather(key_projection_weight, "fsdp", axis=0, tiled=True),
        lax.all_gather(value_projection_weight, "fsdp", axis=0, tiled=True),
        lax.all_gather(w_out, "fsdp", axis=1, tiled=True),
        lax.all_gather(w_gate, "fsdp", axis=0, tiled=True),
        lax.all_gather(w_up, "fsdp", axis=0, tiled=True),
        lax.all_gather(w_down, "fsdp", axis=1, tiled=True),
    )
    seq_count, local_len, model_width = tokens.shape
    sequence_length = segments.shape[1]
    head_dim = query_gain.shape[0]
    q_heads = w_query.shape[1] // head_dim
    kv_heads = key_projection_weight.shape[1] // head_dim
    head_repeats = q_heads // kv_heads
    row_count = seq_count * local_len
    block_share = block_group(seq_count, local_len)
    block_count = seq_count // block_share
    contract_last = (((1,), (1,)), ((), ()))
    contract_first = (((0,), (0,)), ((), ()))
    inv_root = 1.0 / math.sqrt(head_dim)
    row_offset = lax.axis_index("context") * local_len
    positions = doc_positions(segments)
    local_pos = lax.dynamic_slice_in_dim(positions, row_offset, local_len, 1)
    query_segs = lax.dynamic_slice_in_dim(segments, row_offset, local_len, 1)
    rot_cos, rot_sin = rotary_tables(local_pos, head_dim)
    rot_cos = rot_cos.reshape(row_count, 1, head_dim // 2)
    rot_sin = rot_sin.reshape(row_count, 1, head_dim // 2)
    query_idx = row_offset + jnp.arange(local_len, dtype=jnp.int32)
    key_idx = jnp.arange(sequence_length, dtype=jnp.int32)
    causal = key_idx[None, :] <= query_idx[:, None]
    inputs = tokens.reshape(row_count, model_width).astype(jnp.float32)
    in_factor = rms_factor(inputs)
    in_normed = inputs * in_factor
    first_activation = (in_normed * input_gain.astype(jnp.float32)).astype(jnp.bfloat16)
    query_raw = jnp.dot(first_activation, w_query, preferred_element_type=jnp.float32).reshape(
        row_count, q_heads, head_dim
    )
    unrotated_key = jnp.dot(
        first_activation, key_projection_weight, preferred_element_type=jnp.float32
    ).reshape(row_count, kv_heads, head_dim)
    value_reduced = jnp.dot(
        first_activation, value_projection_weight, preferred_element_type=jnp.float32
    ).astype(jnp.bfloat16)
    query_factor = rms_factor(query_raw)
    query_normed = query_raw * query_factor
    query_rot = rotate(query_normed * query_gain.astype(jnp.float32), rot_cos, rot_sin, 1.0).astype(
        jnp.bfloat16
    )
    key_factor = rms_factor(unrotated_key)
    key_normed = unrotated_key * key_factor
    rotary_key = rotate(key_normed * key_gain.astype(jnp.float32), rot_cos, rot_sin, 1.0).astype(
        jnp.bfloat16
    )
    key_view = rotary_key.reshape(seq_count, local_len, kv_heads * head_dim)
    value_view = value_reduced.reshape(seq_count, local_len, kv_heads * head_dim)
    keys_all, values_all = (
        lax.all_gather(key_view, "context", axis=1, tiled=True),
        lax.all_gather(value_view, "context", axis=1, tiled=True),
    )

    def blocked(array):
        return array.reshape((block_count, block_share) + array.shape[1:])

    query_blocks = query_rot.reshape(
        block_count, block_share, local_len, kv_heads, head_repeats, head_dim
    )
    qseg_blocks = blocked(query_segs)
    kseg_blocks = blocked(segments)

    def scores_of(query_part, key_row_matrix, qseg, kseg):
        raw_scores = (
            jnp.einsum(
                "gqkrd,gjkd->gkrqj", query_part, key_row_matrix, preferred_element_type=jnp.float32
            )
            * inv_root
        )
        allowed = (qseg[:, :, None] == kseg[:, None, :]) & causal[None]
        return jnp.where(allowed[:, None, None], raw_scores, MASKED)

    def attend_forward(block_parts):
        query_part, key_part, value_part, qseg, kseg = block_parts
        key_row_matrix = key_part.reshape(block_share, sequence_length, kv_heads, head_dim)
        value_row_matrix = value_part.reshape(block_share, sequence_length, kv_heads, head_dim)
        scores = scores_of(query_part, key_row_matrix, qseg, kseg)
        row_max = jnp.max(scores, axis=-1, keepdims=True)
        weights = jnp.exp(scores - row_max)
        row_total = jnp.sum(weights, axis=-1, keepdims=True)
        attn_probs = (weights / row_total).astype(jnp.bfloat16)
        mixed = jnp.einsum(
            "gkrqj,gjkd->gqkrd", attn_probs, value_row_matrix, preferred_element_type=jnp.float32
        )
        return (mixed.astype(jnp.bfloat16), row_max + jnp.log(row_total))

    mixed, log_total = lax.map(
        attend_forward,
        (query_blocks, blocked(keys_all), blocked(values_all), qseg_blocks, kseg_blocks),
    )
    mixed_flat = mixed.reshape(row_count, q_heads * head_dim)
    attn_part = jnp.dot(mixed_flat, w_out, preferred_element_type=jnp.float32)
    middle_f32 = middle_gain.astype(jnp.float32)
    residual = inputs + lax.psum(attn_part, "tensor")
    mid_factor = rms_factor(residual)
    mid_normed = residual * mid_factor
    act_two = (mid_normed * middle_f32).astype(jnp.bfloat16)
    gate_value = jnp.dot(act_two, w_gate, preferred_element_type=jnp.float32)
    up_value = jnp.dot(act_two, w_up, preferred_element_type=jnp.float32)
    sigmoid_gate = jax.nn.sigmoid(gate_value)
    silu_gate = gate_value * sigmoid_gate
    hidden = (silu_gate * up_value).astype(jnp.bfloat16)
    down_part = jnp.dot(hidden, w_down, preferred_element_type=jnp.float32)
    out_low = (
        residual + lax.psum(down_part.astype(jnp.bfloat16), "tensor").astype(jnp.float32)
    ).astype(jnp.bfloat16)
    grad_low = cotangent.reshape(row_count, model_width)
    d_hidden = lax.dot_general(grad_low, w_down, contract_last, preferred_element_type=jnp.float32)
    g_down = lax.dot_general(hidden, grad_low, contract_first, preferred_element_type=jnp.float32)
    d_gate = (
        d_hidden * up_value * sigmoid_gate * (1.0 + gate_value * (1.0 - sigmoid_gate))
    ).astype(jnp.bfloat16)
    d_up = (d_hidden * silu_gate).astype(jnp.bfloat16)
    g_gate = lax.dot_general(act_two, d_gate, contract_first, preferred_element_type=jnp.float32)
    g_up = lax.dot_general(act_two, d_up, contract_first, preferred_element_type=jnp.float32)
    d_act_part = lax.dot_general(d_gate, w_gate, contract_last, preferred_element_type=jnp.float32)
    d_act_part = d_act_part + lax.dot_general(
        d_up, w_up, contract_last, preferred_element_type=jnp.float32
    )
    d_act_two = lax.psum(d_act_part.astype(jnp.bfloat16), "tensor").astype(jnp.float32)
    g_middle = jnp.sum(d_act_two * mid_normed, axis=0)
    d_residual = grad_low.astype(jnp.float32) + rms_backward(
        d_act_two, mid_normed, mid_factor, middle_f32
    )
    d_res_rows = d_residual.astype(jnp.bfloat16)
    block_out = out_low.reshape(seq_count, local_len, model_width)
    g_out = lax.dot_general(
        mixed_flat, d_res_rows, contract_first, preferred_element_type=jnp.float32
    )
    d_mixed = lax.dot_general(
        d_res_rows, w_out, contract_last, preferred_element_type=jnp.float32
    ).astype(jnp.bfloat16)
    keys_back, values_back = (keys_all, values_all)

    def attend_backward(block_parts):
        query_part, key_part, value_part, qseg, kseg, block_lse, d_part = block_parts
        key_row_matrix = key_part.reshape(block_share, sequence_length, kv_heads, head_dim)
        value_row_matrix = value_part.reshape(block_share, sequence_length, kv_heads, head_dim)
        scores = scores_of(query_part, key_row_matrix, qseg, kseg)
        attn_probs = jnp.exp(scores - block_lse)
        d_probs = jnp.einsum(
            "gqkrd,gjkd->gkrqj", d_part, value_row_matrix, preferred_element_type=jnp.float32
        )
        inner_sum = jnp.sum(attn_probs * d_probs, axis=-1, keepdims=True)
        d_scores = (attn_probs * (d_probs - inner_sum)).astype(jnp.bfloat16)
        d_query = (
            jnp.einsum(
                "gkrqj,gjkd->gqkrd", d_scores, key_row_matrix, preferred_element_type=jnp.float32
            )
            * inv_root
        )
        d_keys = (
            jnp.einsum(
                "gkrqj,gqkrd->gjkd", d_scores, query_part, preferred_element_type=jnp.float32
            )
            * inv_root
        )
        d_values = jnp.einsum(
            "gkrqj,gqkrd->gjkd",
            attn_probs.astype(jnp.bfloat16),
            d_part,
            preferred_element_type=jnp.float32,
        )
        return (
            d_query,
            d_keys.reshape(block_share, sequence_length, kv_heads * head_dim),
            d_values.reshape(block_share, sequence_length, kv_heads * head_dim),
        )

    d_mixed_blocks = d_mixed.reshape(
        block_count, block_share, local_len, kv_heads, head_repeats, head_dim
    )
    d_query, d_keys_full, d_values_full = lax.map(
        attend_backward,
        (
            query_blocks,
            blocked(keys_back),
            blocked(values_back),
            qseg_blocks,
            kseg_blocks,
            log_total,
            d_mixed_blocks,
        ),
    )
    d_keys_full = d_keys_full.reshape(seq_count, sequence_length, kv_heads * head_dim)
    d_values_full = d_values_full.reshape(seq_count, sequence_length, kv_heads * head_dim)
    d_keys, d_values = (
        lax.psum_scatter(
            d_keys_full.astype(jnp.bfloat16), "context", scatter_dimension=1, tiled=True
        ).astype(jnp.float32),
        lax.psum_scatter(
            d_values_full.astype(jnp.bfloat16), "context", scatter_dimension=1, tiled=True
        ).astype(jnp.float32),
    )
    d_query_rot = rotate(d_query.reshape(row_count, q_heads, head_dim), rot_cos, rot_sin, -1.0)
    g_query_gain = jnp.sum(d_query_rot * query_normed, axis=(0, 1))
    d_query_raw = rms_backward(
        d_query_rot, query_normed, query_factor, query_gain.astype(jnp.float32)
    )
    d_query_raw = d_query_raw.astype(jnp.bfloat16).reshape(row_count, q_heads * head_dim)
    d_key_rot = rotate(d_keys.reshape(row_count, kv_heads, head_dim), rot_cos, rot_sin, -1.0)
    g_key_gain = jnp.sum(d_key_rot * key_normed, axis=(0, 1))
    d_key_raw = rms_backward(d_key_rot, key_normed, key_factor, key_gain.astype(jnp.float32))
    d_key_raw = d_key_raw.astype(jnp.bfloat16).reshape(row_count, kv_heads * head_dim)
    d_value_low = d_values.reshape(row_count, kv_heads * head_dim).astype(jnp.bfloat16)
    g_query = lax.dot_general(
        first_activation, d_query_raw, contract_first, preferred_element_type=jnp.float32
    )
    g_key = lax.dot_general(
        first_activation, d_key_raw, contract_first, preferred_element_type=jnp.float32
    )
    g_value = lax.dot_general(
        first_activation, d_value_low, contract_first, preferred_element_type=jnp.float32
    )
    d_first = lax.dot_general(
        d_query_raw, w_query, contract_last, preferred_element_type=jnp.float32
    )
    d_first = d_first + lax.dot_general(
        d_key_raw, key_projection_weight, contract_last, preferred_element_type=jnp.float32
    )
    d_first = d_first + lax.dot_general(
        d_value_low, value_projection_weight, contract_last, preferred_element_type=jnp.float32
    )
    input_f32 = input_gain.astype(jnp.float32)
    d_act_one, g_query_gain, g_key_gain = (
        lax.psum(d_first.astype(jnp.bfloat16), "tensor").astype(jnp.float32),
        lax.psum(g_query_gain.astype(jnp.bfloat16), "tensor").astype(jnp.float32),
        lax.psum(g_key_gain.astype(jnp.bfloat16), "tensor").astype(jnp.float32),
    )
    g_input = jnp.sum(d_act_one * in_normed, axis=0)
    d_inputs = d_residual + rms_backward(d_act_one, in_normed, in_factor, input_f32)
    grad_flat = d_inputs.astype(jnp.bfloat16)
    grad_tokens = grad_flat.reshape(seq_count, local_len, model_width)
    (
        g_input,
        g_middle,
        g_query_gain,
        g_key_gain,
        g_query,
        g_key,
        g_value,
        g_out,
        g_gate,
        g_up,
        g_down,
    ) = (
        lax.psum_scatter(
            g_input.astype(jnp.bfloat16), "fsdp", scatter_dimension=0, tiled=True
        ).astype(jnp.float32),
        lax.psum_scatter(
            g_middle.astype(jnp.bfloat16), "fsdp", scatter_dimension=0, tiled=True
        ).astype(jnp.float32),
        lax.psum_scatter(
            g_query_gain.astype(jnp.bfloat16), "fsdp", scatter_dimension=0, tiled=True
        ).astype(jnp.float32),
        lax.psum_scatter(
            g_key_gain.astype(jnp.bfloat16), "fsdp", scatter_dimension=0, tiled=True
        ).astype(jnp.float32),
        lax.psum_scatter(
            g_query.astype(jnp.bfloat16), "fsdp", scatter_dimension=0, tiled=True
        ).astype(jnp.float32),
        lax.psum_scatter(
            g_key.astype(jnp.bfloat16), "fsdp", scatter_dimension=0, tiled=True
        ).astype(jnp.float32),
        lax.psum_scatter(
            g_value.astype(jnp.bfloat16), "fsdp", scatter_dimension=0, tiled=True
        ).astype(jnp.float32),
        lax.psum_scatter(
            g_out.astype(jnp.bfloat16), "fsdp", scatter_dimension=1, tiled=True
        ).astype(jnp.float32),
        lax.psum_scatter(
            g_gate.astype(jnp.bfloat16), "fsdp", scatter_dimension=0, tiled=True
        ).astype(jnp.float32),
        lax.psum_scatter(g_up.astype(jnp.bfloat16), "fsdp", scatter_dimension=0, tiled=True).astype(
            jnp.float32
        ),
        lax.psum_scatter(
            g_down.astype(jnp.bfloat16), "fsdp", scatter_dimension=1, tiled=True
        ).astype(jnp.float32),
    )
    (
        g_input,
        g_middle,
        g_query_gain,
        g_key_gain,
        g_query,
        g_key,
        g_value,
        g_out,
        g_gate,
        g_up,
        g_down,
    ) = (
        lax.psum(g_input.astype(jnp.bfloat16), "context").astype(jnp.float32),
        lax.psum(g_middle.astype(jnp.bfloat16), "context").astype(jnp.float32),
        lax.psum(g_query_gain.astype(jnp.bfloat16), "context").astype(jnp.float32),
        lax.psum(g_key_gain.astype(jnp.bfloat16), "context").astype(jnp.float32),
        lax.psum(g_query.astype(jnp.bfloat16), "context").astype(jnp.float32),
        lax.psum(g_key.astype(jnp.bfloat16), "context").astype(jnp.float32),
        lax.psum(g_value.astype(jnp.bfloat16), "context").astype(jnp.float32),
        lax.psum(g_out.astype(jnp.bfloat16), "context").astype(jnp.float32),
        lax.psum(g_gate.astype(jnp.bfloat16), "context").astype(jnp.float32),
        lax.psum(g_up.astype(jnp.bfloat16), "context").astype(jnp.float32),
        lax.psum(g_down.astype(jnp.bfloat16), "context").astype(jnp.float32),
    )
    return (
        block_out,
        grad_tokens,
        g_input,
        g_middle,
        g_query_gain,
        g_key_gain,
        g_query,
        g_key,
        g_value,
        g_out,
        g_gate,
        g_up,
        g_down,
    )


def solution(mesh):
    return jax.shard_map(
        local,
        mesh=mesh,
        in_specs=(
            P("fsdp", "context", None),
            P("fsdp", None),
            P("fsdp"),
            P("fsdp"),
            P("fsdp"),
            P("fsdp"),
            P("fsdp", "tensor"),
            P("fsdp", "tensor"),
            P("fsdp", "tensor"),
            P("tensor", "fsdp"),
            P("fsdp", "tensor"),
            P("fsdp", "tensor"),
            P("tensor", "fsdp"),
            P("fsdp", "context", None),
        ),
        out_specs=(
            P("fsdp", "context", None),
            P("fsdp", "context", None),
            P("fsdp"),
            P("fsdp"),
            P("fsdp"),
            P("fsdp"),
            P("fsdp", "tensor"),
            P("fsdp", "tensor"),
            P("fsdp", "tensor"),
            P("tensor", "fsdp"),
            P("fsdp", "tensor"),
            P("fsdp", "tensor"),
            P("tensor", "fsdp"),
        ),
        check_vma=False,
    )
```

profile of v0, /device:TPU:0, one launch (start us, length us, event | category | flops | bytes accessed | tf_op | source)
XLA Modules:
  0.0 2209.5 jit_solution(4531047468539229671)
XLA Ops:
  110.8 111.4 %all-gather.18.cloned.1.call-done = bf16[8,1024,512]{1,0,2:T(8,128)(2,1)} async-done(((bf16[8,256,512]{1,0,2:T(8,128)(2,1)}), bf16[8,1024,512]{1,0,2:T(8,128)(2,1)}) %all-gather.18.cloned.1.call-update) | async-done | bytes 8388624 | tf_op jit(solution)/shard_map/all_gather | solution.py:147
  233.9 137.5 %all-gather.14.cloned.1.call-done = bf16[8,1024,512]{2,1,0:T(8,128)(2,1)} async-done(((bf16[8,256,512]{2,1,0:T(8,128)(2,1)}), bf16[8,1024,512]{2,1,0:T(8,128)(2,1)}) %all-gather.14.cloned.1.call-update) | async-done | bytes 8388624 | tf_op jit(solution)/shard_map/all_gather | solution.py:148
  383.0 142.1 %while.28 = (s32[]{:T(128)}, bf16[4,2,256,4,2,128]{5,4,3,2,1,0:T(2,128)(2,1)}, f32[4,2,4,2,256,1]{4,3,2,1,5,0:T(2,128)}, bf16[4,2,1024,512]{2,3,1,0:T(8,128)(2,1...) while((s32[]{:T(128)}, ...), condition=%wide.region_8.9_spmd.clone, body=%wide.region_5.8_spmd.clone.sunk | while | flops 2199646208 | bytes 71990392 | solution.py:184
  550.9 189.2 %all-reduce.17.cloned.1.call-done = f32[2048,1024]{1,0:T(8,128)} async-done(((f32[2048,1024]{1,0:T(8,128)}), f32[2048,1024]{1,0:T(8,128)}) %all-reduce.17.cloned.1.call-update) | async-done | bytes 8388624 | tf_op jit(solution)/shard_map/psum | solution.py:191
  751.5 19.0 all-gather.26.cloned.1.call-done
  770.6 12.4 fusion.70
  782.9 17.8 all-gather.24.cloned.1.call-done
  800.7 12.3 fusion.69
  813.0 18.0 all-gather.28.cloned.1.call-done
  831.1 24.1 %multiply_convert_fusion = (bf16[2048,1536]{1,0:T(8,128)(2,1)}, bf16[2048,1536]{1,0:T(8,128)(2,1)}, bf16[2048,1536]{1,0:T(8,128)(2,1)}) fusion(f32[2048,1536]{1,0:T(8,128)} %fusion.69, f32[2048,1536]{1,0:T(8,128)} %fusion.70, bf16[2048,1024]{1,0:T(8,128)(2,1)} %bitcast.313, bf16[1536,1024]{1,0:T(8,128)(2,1)} %all-gather.28.cloned.1.call-done), kind=kOutput, calls=%fused_computation.63 | convolution fusion | flops 6489636864 | bytes 51380224 | tf_op jit(solution)/shard_map/dot_general | solution.py:205
  872.6 108.0 %all-reduce.19.cloned.1.call-done = bf16[2048,1024]{1,0:T(8,128)(2,1)} async-done(((bf16[2048,1024]{1,0:T(8,128)(2,1)}), bf16[2048,1024]{1,0:T(8,128)(2,1)}) %all-reduce.19.cloned.1.call-update) | async-done | bytes 4194320 | tf_op jit(solution)/shard_map/psum | solution.py:217
  1009.6 245.1 %while.29 = (s32[]{:T(128)}, f32[4,2,256,4,2,128]{2,1,0,5,4,3:T(2,128)}, bf16[4,2,1024,512]{2,3,1,0:T(8,128)(2,1)}, bf16[4,2,1024,512]{2,3,1,0:T(8,128)(2,1)}, b...) while((s32[]{:T(128)}, ...), condition=%wide.region_16.17_spmd.clone, body=%wide.region_14.16_spmd.clone.sunk | while | flops 5435551744 | bytes 168443056 | solution.py:270
  1356.8 53.8 %reduce-scatter.10.cloned.1.call-done = bf16[8,256,512]{1,0,2:T(8,128)(2,1)} async-done(((bf16[8,1024,512]{1,0,2:T(8,128)(2,1)}), bf16[8,256,512]{1,0,2:T(8,128)(2,1)}) %reduce-scatter.10.cloned.1.call-update) | async-done | bytes 2097168 | tf_op jit(solution)/shard_map/reduce_scatter | solution.py:285
  1419.4 139.0 %reduce-scatter.12.cloned.1.call-done = bf16[8,256,512]{2,1,0:T(8,128)(2,1)} async-done(((bf16[8,1024,512]{2,1,0:T(8,128)(2,1)}), bf16[8,256,512]{2,1,0:T(8,128)(2,1)}) %reduce-scatter.12.cloned.1.call-update) | async-done | bytes 2097168 | tf_op jit(solution)/shard_map/reduce_scatter | solution.py:288
  1577.3 22.3 %reduce-scatter.26.cloned.1.call-done = bf16[1536,256]{1,0:T(8,128)(2,1)} async-done(((bf16[1536,1024]{1,0:T(8,128)(2,1)}), bf16[1536,256]{1,0:T(8,128)(2,1)}) %reduce-scatter.26.cloned.1.call-update) | async-done | bytes 786448 | tf_op jit(solution)/shard_map/reduce_scatter | solution.py:374
  1599.6 40.4 %reduce-scatter.22.cloned.1.call-done = bf16[256,1536]{1,0:T(8,128)(2,1)} async-done(((bf16[1024,1536]{1,0:T(8,128)(2,1)}), bf16[256,1536]{1,0:T(8,128)(2,1)}) %reduce-scatter.22.cloned.1.call-update) | async-done | bytes 786448 | tf_op jit(solution)/shard_map/reduce_scatter | solution.py:368
  1640.0 40.5 %reduce-scatter.24.cloned.1.call-done = bf16[256,1536]{1,0:T(8,128)(2,1)} async-done(((bf16[1024,1536]{1,0:T(8,128)(2,1)}), bf16[256,1536]{1,0:T(8,128)(2,1)}) %reduce-scatter.24.cloned.1.call-update) | async-done | bytes 786448 | tf_op jit(solution)/shard_map/reduce_scatter | solution.py:371
  1680.5 33.9 %reduce-scatter.20.cloned.1.call-done = bf16[1024,256]{1,0:T(8,128)(2,1)} async-done(((bf16[1024,1024]{1,0:T(8,128)(2,1)}), bf16[1024,256]{1,0:T(8,128)(2,1)}) %reduce-scatter.20.cloned.1.call-update) | async-done | bytes 524304 | tf_op jit(solution)/shard_map/reduce_scatter | solution.py:365
  1714.4 34.0 %reduce-scatter.14.cloned.1.call-done = bf16[256,1024]{1,0:T(8,128)(2,1)} async-done(((bf16[1024,1024]{1,0:T(8,128)(2,1)}), bf16[256,1024]{1,0:T(8,128)(2,1)}) %reduce-scatter.14.cloned.1.call-update) | async-done | bytes 524304 | tf_op jit(solution)/shard_map/reduce_scatter | solution.py:356
  1748.4 28.0 %reduce-scatter.18.cloned.1.call-done = bf16[256,512]{1,0:T(8,128)(2,1)} async-done(((bf16[1024,512]{1,0:T(8,128)(2,1)}), bf16[256,512]{1,0:T(8,128)(2,1)}) %reduce-scatter.18.cloned.1.call-update) | async-done | bytes 262160 | tf_op jit(solution)/shard_map/reduce_scatter | solution.py:362
  1776.4 28.0 %reduce-scatter.16.cloned.1.call-done = bf16[256,512]{1,0:T(8,128)(2,1)} async-done(((bf16[1024,512]{1,0:T(8,128)(2,1)}), bf16[256,512]{1,0:T(8,128)(2,1)}) %reduce-scatter.16.cloned.1.call-update) | async-done | bytes 262160 | tf_op jit(solution)/shard_map/reduce_scatter | solution.py:359
  1828.9 127.3 %all-reduce.21.cloned.1.call-done = (bf16[256,1024]{1,0:T(8,128)(2,1)}, bf16[256,512]{1,0:T(8,128)(2,1)}, bf16[256,512]{1,0:T(8,128)(2,1)}, bf16[1024,256]{1,0:T...) async-done(((bf16[256,1024]{1,0:T(8,128)(2,1)}, bf16[256,512]{1,0:T(8,128)(2,1)}, bf16[256,512]{1,0:T(8,128)(2,1)}, ...) | async-done | bytes 3932176 | tf_op jit(solution)/shard_map/psum | solution.py:395
  1968.1 188.5 %all-reduce.23.cloned.1.call-done = (bf16[2048,1024]{1,0:T(8,128)(2,1)}, bf16[2048,1024]{1,0:T(8,128)(2,1)}) async-done(((bf16[2048,1024]{1,0:T(8,128)(2,1)}, bf16[2048,1024]{1,0:T(8,128)(2,1)}), (bf16[2048,1024]{1,0:T(8,128)(2,1)}, bf16[2048,1024]{1,0:T(8,128)(2,1)})) %all-reduce.23.cloned.1.call-update) | async-done | bytes 8388624 | tf_op jit(solution)/shard_map/psum | solution.py:202
  2188.0 14.3 fusion.46
  (368 shorter events, 791.4 us)
Async XLA Ops:
  7.2 33.7 %all-gather.16.cloned.1.call-start = ((), (), s32[]{:S(2)}) async-start(), calls=%async_computation.11 | async-start | bytes 1310720 | tf_op jit(solution)/shard_map/all_gather | solution.py:92
  7.9 48.5 %all-gather.12.cloned.1.call-start = ((), (), s32[]{:S(2)}) async-start(), calls=%async_computation.9 | async-start | bytes 1310720 | tf_op jit(solution)/shard_map/all_gather | solution.py:93
  8.7 62.9 %all-gather.20.cloned.1.call-start = ((), (), s32[]{:S(2)}) async-start(), calls=%async_computation.13 | async-start | bytes 2621440 | tf_op jit(solution)/shard_map/all_gather | solution.py:91
  9.4 212.7 %all-gather.18.cloned.1.call-start = ((), (), s32[]{:S(2)}) async-start(), calls=%async_computation.12 | async-start | bytes 10485760 | tf_op jit(solution)/shard_map/all_gather | solution.py:147
  52.2 319.2 %all-gather.14.cloned.1.call-start = ((), (), s32[]{:S(2)}) async-start(), calls=%async_computation.10 | async-start | bytes 10485760 | tf_op jit(solution)/shard_map/all_gather | solution.py:148
  62.8 470.2 %all-gather.22.cloned.1.call-start = ((), (), s32[]{:S(2)}) async-start(), calls=%async_computation.14 | async-start | bytes 2621440 | tf_op jit(solution)/shard_map/all_gather | solution.py:94
  63.4 676.7 %all-reduce.17.cloned.1.call-start = ((), (), s32[]{:S(2)}) async-start(), calls=%async_computation.15 | async-start | bytes 16777216 | tf_op jit(solution)/shard_map/psum | solution.py:191
  543.7 226.9 %all-gather.26.cloned.1.call-start = ((), (), s32[]{:S(2)}) async-start(), calls=%async_computation.17 | async-start | bytes 3932160 | tf_op jit(solution)/shard_map/all_gather | solution.py:96
  544.5 256.2 %all-gather.24.cloned.1.call-start = ((), (), s32[]{:S(2)}) async-start(), calls=%async_computation.16 | async-start | bytes 3932160 | tf_op jit(solution)/shard_map/all_gather | solution.py:95
  545.2 285.9 %all-gather.28.cloned.1.call-start = ((), (), s32[]{:S(2)}) async-start(), calls=%async_computation.18 | async-start | bytes 3932160 | tf_op jit(solution)/shard_map/all_gather | solution.py:97
  545.8 434.7 %all-reduce.19.cloned.1.call-start = ((), (), s32[]{:S(2)}) async-start(), calls=%async_computation.19 | async-start | bytes 8388608 | tf_op jit(solution)/shard_map/psum | solution.py:217
  872.5 538.2 %reduce-scatter.10.cloned.1.call-start = ((), (), s32[]{:S(2)}) async-start(), calls=%async_computation.20 | async-start | bytes 10485760 | tf_op jit(solution)/shard_map/reduce_scatter | solution.py:285
  1266.1 292.3 %reduce-scatter.12.cloned.1.call-start = ((), (), s32[]{:S(2)}) async-start(), calls=%async_computation.21 | async-start | bytes 10485760 | tf_op jit(solution)/shard_map/reduce_scatter | solution.py:288
  1277.8 321.8 %reduce-scatter.26.cloned.1.call-start = ((), (), s32[]{:S(2)}) async-start(), calls=%async_computation.28 | async-start | bytes 3932160 | tf_op jit(solution)/shard_map/reduce_scatter | solution.py:374
  1289.1 350.9 %reduce-scatter.22.cloned.1.call-start = ((), (), s32[]{:S(2)}) async-start(), calls=%async_computation.26 | async-start | bytes 3932160 | tf_op jit(solution)/shard_map/reduce_scatter | solution.py:368
  1300.6 379.9 %reduce-scatter.24.cloned.1.call-start = ((), (), s32[]{:S(2)}) async-start(), calls=%async_computation.27 | async-start | bytes 3932160 | tf_op jit(solution)/shard_map/reduce_scatter | solution.py:371
  1312.6 401.8 %reduce-scatter.20.cloned.1.call-start = ((), (), s32[]{:S(2)}) async-start(), calls=%async_computation.25 | async-start | bytes 2621440 | tf_op jit(solution)/shard_map/reduce_scatter | solution.py:365
  1323.2 425.1 %reduce-scatter.14.cloned.1.call-start = ((), (), s32[]{:S(2)}) async-start(), calls=%async_computation.22 | async-start | bytes 2621440 | tf_op jit(solution)/shard_map/reduce_scatter | solution.py:356
  1356.8 419.6 %reduce-scatter.18.cloned.1.call-start = ((), (), s32[]{:S(2)}) async-start(), calls=%async_computation.24 | async-start | bytes 1310720 | tf_op jit(solution)/shard_map/reduce_scatter | solution.py:362
  1564.6 239.8 %reduce-scatter.16.cloned.1.call-start = ((), (), s32[]{:S(2)}) async-start(), calls=%async_computation.23 | async-start | bytes 1310720 | tf_op jit(solution)/shard_map/reduce_scatter | solution.py:359
  1577.2 378.9 %all-reduce.21.cloned.1.call-start = ((), (), s32[]{:S(2)}) async-start(), calls=%async_computation.29 | async-start | bytes 7864320 | tf_op jit(solution)/shard_map/psum | solution.py:395
  1804.5 352.1 %all-reduce.23.cloned.1.call-start = ((), (), s32[]{:S(2)}) async-start(), calls=%async_computation.30 | async-start | bytes 16777216 | tf_op jit(solution)/shard_map/psum | solution.py:202
  1962.1 194.5 %copy-start.30 = (f32[1,2,8,128]{3,1,2,0:T(2,128)S(1)}, f32[1,2,8,128]{3,1,2,0:T(2,128)}, u32[]{:S(2)}) copy-start(f32[1,2,8,128]{3,1,2,0:T(2,128)} %copy-done.29) | copy-start | bytes 24580
  1962.1 194.5 %copy-start.34 = (f32[4,1,256]{2,1,0:T(1,128)S(1)}, f32[4,1,256]{2,1,0:T(1,128)}, u32[]{:S(2)}) copy-start(f32[4,1,256]{2,1,0:T(1,128)} %copy-done.33) | copy-start | bytes 12292
  (46 other events, 680.0 us)
Sparse Core Ops, SparseCore 0:
  9.6 19.4 all-gather.15
  30.6 16.7 all-gather.11
  48.9 22.5 all-gather.19
  73.0 149.1 all-gather.17
  223.6 147.8 all-gather.13
  372.8 21.0 all-gather.21
  543.8 196.2 all-reduce.16
  741.7 28.8 all-gather.25
  772.1 28.5 all-gather.23
  802.1 28.9 all-gather.27
  872.6 107.8 all-reduce.18
  1266.2 144.4 reduce-scatter.9
  1413.2 145.1 reduce-scatter.11
  1560.9 38.6 reduce-scatter.25
  1602.0 37.9 reduce-scatter.21
  1642.6 37.9 reduce-scatter.23
  1682.9 31.4 reduce-scatter.19
  1716.9 31.3 reduce-scatter.13
  1751.5 24.8 reduce-scatter.17
  1779.5 24.8 reduce-scatter.15
  1807.4 148.7 all-reduce.20
  1959.2 197.2 all-reduce.22
where the time goes:
time: 2220 us; the launch traced here: 2210 us
  waiting for transfers between devices  1350 us (61%)
  matrix products  399 us (18%)
  local copies, waits for them, and re-layouts  200 us (9%)
  other arithmetic  200 us (9%)
  blocking collectives  42 us (2%)
    psum x1, waiting for transfers between devices, local(): residual = inputs + lax.psum(attn_part, 'tensor')  189 us
    psum x1, waiting for transfers between devices, local(): lax.psum(down_part.astype(jnp.bfloat16), 'tensor').astype(jnp.float32)  188 us
    reduce_scatter x1, waiting for transfers between devices, local(): lax.psum_scatter(d_values_full.astype(jnp.bfloat16), 'context', scatter_d...  139 us
    all_gather x1, waiting for transfers between devices, local(): lax.all_gather(value_view, 'context', axis=1, tiled=True)  137 us
    psum x1, waiting for transfers between devices, local(): lax.psum(g_query.astype(jnp.bfloat16), 'context').astype(jnp.float32)  127 us
    all_gather x1, waiting for transfers between devices, local(): lax.all_gather(key_view, 'context', axis=1, tiled=True)  111 us
    psum x1, waiting for transfers between devices, local(): lax.psum(d_act_part.astype(jnp.bfloat16), 'tensor').astype(jnp.float32)  108 us
    dot_general x8, matrix products, scores_of(): jnp.einsum('gqkrd,gjkd->gkrqj', query_part, key_row_matrix, preferred_ele...  72.2 us
  transfers between devices with their start and end apart: 22, of which 19 were waited for; matrix products, arithmetic and copies ran while one was open for 19% of the time, Pallas kernels for 0%

commit v1 on v0

--- a/solution.py
+++ b/solution.py
@@ -22,9 +22,8 @@
 def doc_positions(segments):
     sequence_length = segments.shape[-1]
     places = jnp.arange(sequence_length, dtype=jnp.int32)
-    earlier = jnp.concatenate([segments[:, :1], segments[:, :-1]], axis=1)
-    starts = jnp.where(segments != earlier, places[None, :], 0)
-    return places[None, :] - lax.cummax(starts, axis=1)
+    lower = segments[:, None, :] < segments[:, :, None]
+    return places[None, :] - jnp.sum(lower.astype(jnp.int32), axis=-1)
 
 
 def rotary_tables(positions, head_dim):

time: 2220 us -> 2220 us (level)
  no operation moved by 1% of the time
where the time goes in v1:
time: 2220 us; the launch traced here: 2210 us
  waiting for transfers between devices  1350 us (61%)
  matrix products  399 us (18%)
  other arithmetic  201 us (9%)
  local copies, waits for them, and re-layouts  199 us (9%)
  blocking collectives  42 us (2%)
    psum x1, waiting for transfers between devices, local(): residual = inputs + lax.psum(attn_part, 'tensor')  189 us
    psum x1, waiting for transfers between devices, local(): lax.psum(down_part.astype(jnp.bfloat16), 'tensor').astype(jnp.float32)  188 us
    reduce_scatter x1, waiting for transfers between devices, local(): lax.psum_scatter(d_values_full.astype(jnp.bfloat16), 'context', scatter_d...  139 us
    all_gather x1, waiting for transfers between devices, local(): lax.all_gather(value_view, 'context', axis=1, tiled=True)  137 us
    psum x1, waiting for transfers between devices, local(): lax.psum(g_query.astype(jnp.bfloat16), 'context').astype(jnp.float32)  127 us
    all_gather x1, waiting for transfers between devices, local(): lax.all_gather(key_view, 'context', axis=1, tiled=True)  111 us
    psum x1, waiting for transfers between devices, local(): lax.psum(d_act_part.astype(jnp.bfloat16), 'tensor').astype(jnp.float32)  108 us
    dot_general x8, matrix products, scores_of(): jnp.einsum('gqkrd,gjkd->gkrqj', query_part, key_row_matrix, preferred_ele...  72 us
  transfers between devices with their start and end apart: 22, of which 19 were waited for; matrix products, arithmetic and copies ran while one was open for 19% of the time, Pallas kernels for 0%

profile of v1, /device:TPU:0, one launch (start us, length us, event | category | flops | bytes accessed | tf_op | source)
XLA Modules:
  0.0 2209.4 jit_solution(18308302340419063848)
XLA Ops:
  110.7 111.4 %all-gather.18.cloned.1.call-done = bf16[8,1024,512]{1,0,2:T(8,128)(2,1)} async-done(((bf16[8,256,512]{1,0,2:T(8,128)(2,1)}), bf16[8,1024,512]{1,0,2:T(8,128)(2,1)}) %all-gather.18.cloned.1.call-update) | async-done | bytes 8388624 | tf_op jit(solution)/shard_map/all_gather | solution.py:146
  233.9 137.5 %all-gather.14.cloned.1.call-done = bf16[8,1024,512]{2,1,0:T(8,128)(2,1)} async-done(((bf16[8,256,512]{2,1,0:T(8,128)(2,1)}), bf16[8,1024,512]{2,1,0:T(8,128)(2,1)}) %all-gather.14.cloned.1.call-update) | async-done | bytes 8388624 | tf_op jit(solution)/shard_map/all_gather | solution.py:147
  383.0 141.8 %while.28 = (s32[]{:T(128)}, bf16[4,2,256,4,2,128]{5,4,3,2,1,0:T(2,128)(2,1)}, f32[4,2,4,2,256,1]{4,3,2,1,5,0:T(2,128)}, bf16[4,2,1024,512]{2,3,1,0:T(8,128)(2,1...) while((s32[]{:T(128)}, ...), condition=%wide.region_7.8_spmd.clone, body=%wide.region_4.7_spmd.clone.sunk | while | flops 2199646208 | bytes 71990392 | solution.py:183
  550.6 189.2 %all-reduce.17.cloned.1.call-done = f32[2048,1024]{1,0:T(8,128)} async-done(((f32[2048,1024]{1,0:T(8,128)}), f32[2048,1024]{1,0:T(8,128)}) %all-reduce.17.cloned.1.call-update) | async-done | bytes 8388624 | tf_op jit(solution)/shard_map/psum | solution.py:190
  751.3 19.0 all-gather.26.cloned.1.call-done
  770.3 12.4 fusion.70
  782.7 17.7 all-gather.24.cloned.1.call-done
  800.4 12.3 fusion.69
  812.8 18.0 all-gather.28.cloned.1.call-done
  830.8 24.1 %multiply_convert_fusion = (bf16[2048,1536]{1,0:T(8,128)(2,1)}, bf16[2048,1536]{1,0:T(8,128)(2,1)}, bf16[2048,1536]{1,0:T(8,128)(2,1)}) fusion(f32[2048,1536]{1,0:T(8,128)} %fusion.69, f32[2048,1536]{1,0:T(8,128)} %fusion.70, bf16[2048,1024]{1,0:T(8,128)(2,1)} %bitcast.304, bf16[1536,1024]{1,0:T(8,128)(2,1)} %all-gather.28.cloned.1.call-done), kind=kOutput, calls=%fused_computation.64 | convolution fusion | flops 6489636864 | bytes 51380224 | tf_op jit(solution)/shard_map/dot_general | solution.py:204
  872.3 108.0 %all-reduce.19.cloned.1.call-done = bf16[2048,1024]{1,0:T(8,128)(2,1)} async-done(((bf16[2048,1024]{1,0:T(8,128)(2,1)}), bf16[2048,1024]{1,0:T(8,128)(2,1)}) %all-reduce.19.cloned.1.call-update) | async-done | bytes 4194320 | tf_op jit(solution)/shard_map/psum | solution.py:216
  1009.3 245.1 %while.29 = (s32[]{:T(128)}, f32[4,2,256,4,2,128]{2,1,0,5,4,3:T(2,128)}, bf16[4,2,1024,512]{2,3,1,0:T(8,128)(2,1)}, bf16[4,2,1024,512]{2,3,1,0:T(8,128)(2,1)}, b...) while((s32[]{:T(128)}, ...), condition=%wide.region_15.16_spmd.clone, body=%wide.region_13.15_spmd.clone.sunk | while | flops 5435551744 | bytes 168443056 | solution.py:269
  1356.6 53.9 %reduce-scatter.10.cloned.1.call-done = bf16[8,256,512]{1,0,2:T(8,128)(2,1)} async-done(((bf16[8,1024,512]{1,0,2:T(8,128)(2,1)}), bf16[8,256,512]{1,0,2:T(8,128)(2,1)}) %reduce-scatter.10.cloned.1.call-update) | async-done | bytes 2097168 | tf_op jit(solution)/shard_map/reduce_scatter | solution.py:284
  1419.2 139.0 %reduce-scatter.12.cloned.1.call-done = bf16[8,256,512]{2,1,0:T(8,128)(2,1)} async-done(((bf16[8,1024,512]{2,1,0:T(8,128)(2,1)}), bf16[8,256,512]{2,1,0:T(8,128)(2,1)}) %reduce-scatter.12.cloned.1.call-update) | async-done | bytes 2097168 | tf_op jit(solution)/shard_map/reduce_scatter | solution.py:287
  1577.1 22.3 %reduce-scatter.26.cloned.1.call-done = bf16[1536,256]{1,0:T(8,128)(2,1)} async-done(((bf16[1536,1024]{1,0:T(8,128)(2,1)}), bf16[1536,256]{1,0:T(8,128)(2,1)}) %reduce-scatter.26.cloned.1.call-update) | async-done | bytes 786448 | tf_op jit(solution)/shard_map/reduce_scatter | solution.py:373
  1599.4 40.4 %reduce-scatter.22.cloned.1.call-done = bf16[256,1536]{1,0:T(8,128)(2,1)} async-done(((bf16[1024,1536]{1,0:T(8,128)(2,1)}), bf16[256,1536]{1,0:T(8,128)(2,1)}) %reduce-scatter.22.cloned.1.call-update) | async-done | bytes 786448 | tf_op jit(solution)/shard_map/reduce_scatter | solution.py:367
  1639.8 40.5 %reduce-scatter.24.cloned.1.call-done = bf16[256,1536]{1,0:T(8,128)(2,1)} async-done(((bf16[1024,1536]{1,0:T(8,128)(2,1)}), bf16[256,1536]{1,0:T(8,128)(2,1)}) %reduce-scatter.24.cloned.1.call-update) | async-done | bytes 786448 | tf_op jit(solution)/shard_map/reduce_scatter | solution.py:370
  1680.3 33.9 %reduce-scatter.20.cloned.1.call-done = bf16[1024,256]{1,0:T(8,128)(2,1)} async-done(((bf16[1024,1024]{1,0:T(8,128)(2,1)}), bf16[1024,256]{1,0:T(8,128)(2,1)}) %reduce-scatter.20.cloned.1.call-update) | async-done | bytes 524304 | tf_op jit(solution)/shard_map/reduce_scatter | solution.py:364
  1714.2 34.0 %reduce-scatter.14.cloned.1.call-done = bf16[256,1024]{1,0:T(8,128)(2,1)} async-done(((bf16[1024,1024]{1,0:T(8,128)(2,1)}), bf16[256,1024]{1,0:T(8,128)(2,1)}) %reduce-scatter.14.cloned.1.call-update) | async-done | bytes 524304 | tf_op jit(solution)/shard_map/reduce_scatter | solution.py:355
  1748.2 28.0 %reduce-scatter.18.cloned.1.call-done = bf16[256,512]{1,0:T(8,128)(2,1)} async-done(((bf16[1024,512]{1,0:T(8,128)(2,1)}), bf16[256,512]{1,0:T(8,128)(2,1)}) %reduce-scatter.18.cloned.1.call-update) | async-done | bytes 262160 | tf_op jit(solution)/shard_map/reduce_scatter | solution.py:361
  1776.2 28.1 %reduce-scatter.16.cloned.1.call-done = bf16[256,512]{1,0:T(8,128)(2,1)} async-done(((bf16[1024,512]{1,0:T(8,128)(2,1)}), bf16[256,512]{1,0:T(8,128)(2,1)}) %reduce-scatter.16.cloned.1.call-update) | async-done | bytes 262160 | tf_op jit(solution)/shard_map/reduce_scatter | solution.py:358
  1828.7 127.2 %all-reduce.21.cloned.1.call-done = (bf16[256,1024]{1,0:T(8,128)(2,1)}, bf16[256,512]{1,0:T(8,128)(2,1)}, bf16[256,512]{1,0:T(8,128)(2,1)}, bf16[1024,256]{1,0:T...) async-done(((bf16[256,1024]{1,0:T(8,128)(2,1)}, bf16[256,512]{1,0:T(8,128)(2,1)}, bf16[256,512]{1,0:T(8,128)(2,1)}, ...) | async-done | bytes 3932176 | tf_op jit(solution)/shard_map/psum | solution.py:394
  1967.9 188.5 %all-reduce.23.cloned.1.call-done = (bf16[2048,1024]{1,0:T(8,128)(2,1)}, bf16[2048,1024]{1,0:T(8,128)(2,1)}) async-done(((bf16[2048,1024]{1,0:T(8,128)(2,1)}, bf16[2048,1024]{1,0:T(8,128)(2,1)}), (bf16[2048,1024]{1,0:T(8,128)(2,1)}, bf16[2048,1024]{1,0:T(8,128)(2,1)})) %all-reduce.23.cloned.1.call-update) | async-done | bytes 8388624 | tf_op jit(solution)/shard_map/psum | solution.py:201
  2187.8 14.3 fusion.46
  (361 shorter events, 791.1 us)
Async XLA Ops:
  7.2 34.6 %all-gather.16.cloned.1.call-start = ((), (), s32[]{:S(2)}) async-start(), calls=%async_computation.11 | async-start | bytes 1310720 | tf_op jit(solution)/shard_map/all_gather | solution.py:91
  7.9 49.5 %all-gather.12.cloned.1.call-start = ((), (), s32[]{:S(2)}) async-start(), calls=%async_computation.9 | async-start | bytes 1310720 | tf_op jit(solution)/shard_map/all_gather | solution.py:92
  8.7 62.9 %all-gather.20.cloned.1.call-start = ((), (), s32[]{:S(2)}) async-start(), calls=%async_computation.13 | async-start | bytes 2621440 | tf_op jit(solution)/shard_map/all_gather | solution.py:90
  9.4 212.7 %all-gather.18.cloned.1.call-start = ((), (), s32[]{:S(2)}) async-start(), calls=%async_computation.12 | async-start | bytes 10485760 | tf_op jit(solution)/shard_map/all_gather | solution.py:146
  53.1 318.3 %all-gather.14.cloned.1.call-start = ((), (), s32[]{:S(2)}) async-start(), calls=%async_computation.10 | async-start | bytes 10485760 | tf_op jit(solution)/shard_map/all_gather | solution.py:147
  63.7 469.0 %all-gather.22.cloned.1.call-start = ((), (), s32[]{:S(2)}) async-start(), calls=%async_computation.14 | async-start | bytes 2621440 | tf_op jit(solution)/shard_map/all_gather | solution.py:93
  64.3 675.6 %all-reduce.17.cloned.1.call-start = ((), (), s32[]{:S(2)}) async-start(), calls=%async_computation.15 | async-start | bytes 16777216 | tf_op jit(solution)/shard_map/psum | solution.py:190
  543.4 226.9 %all-gather.26.cloned.1.call-start = ((), (), s32[]{:S(2)}) async-start(), calls=%async_computation.17 | async-start | bytes 3932160 | tf_op jit(solution)/shard_map/all_gather | solution.py:95
  544.2 256.3 %all-gather.24.cloned.1.call-start = ((), (), s32[]{:S(2)}) async-start(), calls=%async_computation.16 | async-start | bytes 3932160 | tf_op jit(solution)/shard_map/all_gather | solution.py:94
  544.9 285.9 %all-gather.28.cloned.1.call-start = ((), (), s32[]{:S(2)}) async-start(), calls=%async_computation.18 | async-start | bytes 3932160 | tf_op jit(solution)/shard_map/all_gather | solution.py:96
  545.5 434.8 %all-reduce.19.cloned.1.call-start = ((), (), s32[]{:S(2)}) async-start(), calls=%async_computation.19 | async-start | bytes 8388608 | tf_op jit(solution)/shard_map/psum | solution.py:216
  872.2 538.2 %reduce-scatter.10.cloned.1.call-start = ((), (), s32[]{:S(2)}) async-start(), calls=%async_computation.20 | async-start | bytes 10485760 | tf_op jit(solution)/shard_map/reduce_scatter | solution.py:284
  1265.8 292.4 %reduce-scatter.12.cloned.1.call-start = ((), (), s32[]{:S(2)}) async-start(), calls=%async_computation.21 | async-start | bytes 10485760 | tf_op jit(solution)/shard_map/reduce_scatter | solution.py:287
  1277.6 321.8 %reduce-scatter.26.cloned.1.call-start = ((), (), s32[]{:S(2)}) async-start(), calls=%async_computation.28 | async-start | bytes 3932160 | tf_op jit(solution)/shard_map/reduce_scatter | solution.py:373
  1288.9 350.9 %reduce-scatter.22.cloned.1.call-start = ((), (), s32[]{:S(2)}) async-start(), calls=%async_computation.26 | async-start | bytes 3932160 | tf_op jit(solution)/shard_map/reduce_scatter | solution.py:367
  1300.4 379.9 %reduce-scatter.24.cloned.1.call-start = ((), (), s32[]{:S(2)}) async-start(), calls=%async_computation.27 | async-start | bytes 3932160 | tf_op jit(solution)/shard_map/reduce_scatter | solution.py:370
  1312.3 401.8 %reduce-scatter.20.cloned.1.call-start = ((), (), s32[]{:S(2)}) async-start(), calls=%async_computation.25 | async-start | bytes 2621440 | tf_op jit(solution)/shard_map/reduce_scatter | solution.py:364
  1323.0 425.2 %reduce-scatter.14.cloned.1.call-start = ((), (), s32[]{:S(2)}) async-start(), calls=%async_computation.22 | async-start | bytes 2621440 | tf_op jit(solution)/shard_map/reduce_scatter | solution.py:355
  1356.6 419.7 %reduce-scatter.18.cloned.1.call-start = ((), (), s32[]{:S(2)}) async-start(), calls=%async_computation.24 | async-start | bytes 1310720 | tf_op jit(solution)/shard_map/reduce_scatter | solution.py:361
  1564.4 239.9 %reduce-scatter.16.cloned.1.call-start = ((), (), s32[]{:S(2)}) async-start(), calls=%async_computation.23 | async-start | bytes 1310720 | tf_op jit(solution)/shard_map/reduce_scatter | solution.py:358
  1577.0 378.9 %all-reduce.21.cloned.1.call-start = ((), (), s32[]{:S(2)}) async-start(), calls=%async_computation.29 | async-start | bytes 7864320 | tf_op jit(solution)/shard_map/psum | solution.py:394
  1804.3 352.1 %all-reduce.23.cloned.1.call-start = ((), (), s32[]{:S(2)}) async-start(), calls=%async_computation.30 | async-start | bytes 16777216 | tf_op jit(solution)/shard_map/psum | solution.py:201
  1961.9 194.5 %copy-start.30 = (f32[1,2,8,128]{3,1,2,0:T(2,128)S(1)}, f32[1,2,8,128]{3,1,2,0:T(2,128)}, u32[]{:S(2)}) copy-start(f32[1,2,8,128]{3,1,2,0:T(2,128)} %copy-done.29) | copy-start | bytes 24580
  1961.9 194.5 %copy-start.34 = (f32[4,1,256]{2,1,0:T(1,128)S(1)}, f32[4,1,256]{2,1,0:T(1,128)}, u32[]{:S(2)}) copy-start(f32[4,1,256]{2,1,0:T(1,128)} %copy-done.33) | copy-start | bytes 12292
  (46 other events, 679.4 us)
Sparse Core Ops, SparseCore 0:
  9.6 19.4 all-gather.15
  30.6 16.7 all-gather.11
  48.9 22.5 all-gather.19
  73.0 149.1 all-gather.17
  223.6 147.8 all-gather.13
  372.8 21.0 all-gather.21
  543.5 196.2 all-reduce.16
  741.4 28.8 all-gather.25
  771.8 28.5 all-gather.23
  801.8 28.9 all-gather.27
  872.3 107.8 all-reduce.18
  1266.0 144.4 reduce-scatter.9
  1412.9 145.2 reduce-scatter.11
  1560.7 38.6 reduce-scatter.25
  1601.8 37.9 reduce-scatter.21
  1642.3 37.9 reduce-scatter.23
  1682.7 31.4 reduce-scatter.19
  1716.7 31.4 reduce-scatter.13
  1751.3 24.8 reduce-scatter.17
  1779.3 24.9 reduce-scatter.15
  1807.2 148.6 all-reduce.20
  1959.1 197.2 all-reduce.22
